TPU v7x, 32 devices: a whole 2x2x4 slice. The times are simulated.
32 devices in a mesh: row: 8 (over z, y), col: 4 (over x, core).
Axes of the slice: x: 2, y: 2, z: 4, core: 2. Of those that a mesh axis runs over, the one named last changes fastest.
Arguments:
- panel_block: float32 [16384, 128], P(('row', 'col')), may hold values from -360 to 360
- trailing: float32 [16384, 2048], P('row', 'col'), may hold values from -2048 to 2048
Outputs:
- r_scaled: float32 [128, 128], replicated
- w_scaled: float32 [128, 2048], P(None, 'col')
- remainder: float32 [16384, 2048], P('row', 'col')
All inputs are finite; a program needn't handle non-finite values.
Results may differ from a plain program's by a relative error of at most 0.0003.
Values sent between devices are 32-bit elements; how exact they have to be, the bound alone decides.
No kernel may reach another device: no remote copies, remote signals or barrier semaphores. Data moves between devices by JAX's collectives and lax.ppermute only.
A program may use at most 64 MiB of HBM per device.

v0:
```python
import math
import jax
import jax.numpy as jnp
from jax import lax
from jax.sharding import PartitionSpec as P


def inner_rows(first_block, second_block):
    return jnp.einsum("rk,rc->kc", first_block, second_block, precision=lax.Precision.HIGHEST)


def upper_factor(gram):
    width = gram.shape[0]
    positions = lax.iota(jnp.int32, width)

    def column_step(index, state):
        remaining, lower = state
        picker = (positions == index).astype(jnp.float32)
        column = jnp.dot(remaining, picker, precision=lax.Precision.HIGHEST)
        pivot = jnp.sum(column * picker)
        column = jnp.where(positions >= index, column / jnp.sqrt(pivot), 0.0)
        remaining = remaining - column[:, None] * column[None, :]
        lower = lower + column[:, None] * picker[None, :]
        return (remaining, lower)

    start = (gram, jnp.zeros_like(gram))
    remaining, lower = lax.fori_loop(0, width, column_step, start)
    return lower.T


def upper_inverse(factor):
    width = factor.shape[0]
    positions = lax.iota(jnp.int32, width)

    def row_step(count, inverse):
        index = width - 1 - count
        picker = (positions == index).astype(jnp.float32)
        factor_row = jnp.dot(picker, factor, precision=lax.Precision.HIGHEST)
        pivot = jnp.sum(factor_row * picker)
        new_row = (picker - jnp.dot(factor_row, inverse, precision=lax.Precision.HIGHEST)) / pivot
        return inverse + picker[:, None] * new_row[None, :]

    return lax.fori_loop(0, width, row_step, jnp.zeros_like(factor))


def body(panel_block, trailing):
    total_rows = panel_block.shape[0] * lax.axis_size("row") * lax.axis_size("col")
    norm_scale = 1.0 / math.sqrt(total_rows)
    gathered = lax.all_gather(panel_block, "col", axis=0, tiled=True)
    cross = lax.psum(inner_rows(gathered, trailing), "row")
    local_gram = inner_rows(panel_block, panel_block)
    gram = lax.psum(local_gram, ("row", "col"))
    factor = upper_factor(gram)
    inverse = upper_inverse(factor)
    weights = jnp.dot(inverse.T, cross, precision=lax.Precision.HIGHEST)
    coeffs = jnp.dot(inverse, weights, precision=lax.Precision.HIGHEST)
    remainder = trailing - jnp.dot(gathered, coeffs, precision=lax.Precision.HIGHEST)
    return (factor * norm_scale, weights * norm_scale, remainder)


def solution(mesh):
    in_specs = (P(("row", "col"), None), P("row", "col"))
    out_specs = (P(), P(None, "col"), P("row", "col"))
    return jax.shard_map(body, mesh=mesh, in_specs=in_specs, out_specs=out_specs, check_vma=False)
```

profile of v0, /device:TPU:1, one launch (start us, length us, event | category | flops | bytes accessed | tf_op | source)
XLA Modules:
  0.0 887.3 jit_solution(7918090243251540799)
XLA Ops:
  8.0 2.3 fusion.21
  11.0 5.3 copy.6
  16.3 126.2 %all-reduce.3.cloned.1.call-done = f32[128,128]{1,0:T(8,128)} async-done(((f32[128,128]{1,0:T(8,128)}), f32[128,128]{1,0:T(8,128)}) %all-reduce.3.cloned.1.call-update) | async-done | bytes 65552 | tf_op jit(solution)/shard_map/psum | solution.py:52
  142.5 499.0 %while.32 = (s32[]{:T(128)}, f32[128,128]{1,0:T(8,128)}, f32[128,128]{1,0:T(8,128)S(1)}, s32[]{:T(128)}, s32[]{:T(128)}) while((s32[]{:T(128)}, f32[128,128]{1,0:T(8,128)}, f32[128,128]{1,0:T(8,128)S(1)}, s32[]{:T(128)}, s32[]{:T(128)}) %tuple.77), condition=%wide.region_3.4_spmd.clone.clone, body=%wide.region_1.3_spmd.clone.clone.sunk | while | flops 279682 | bytes 330859 | solution.py:27
  142.5 1.6 fusion.53
  146.4 1.6 fusion.53
  150.3 1.6 fusion.53
  154.2 1.6 fusion.53
  158.1 1.6 fusion.53
  165.9 1.6 fusion.53
  169.8 1.6 fusion.53
  173.7 1.6 fusion.53
  177.6 1.6 fusion.53
  181.5 1.6 fusion.53
  185.4 1.6 fusion.53
  189.3 1.6 fusion.53
  193.2 1.6 fusion.53
  197.1 1.6 fusion.53
  201.0 1.6 fusion.53
  204.9 1.6 fusion.53
  208.8 1.6 fusion.53
  212.7 1.6 fusion.53
  216.6 1.6 fusion.53
  220.5 1.6 fusion.53
  224.4 1.6 fusion.53
  228.3 1.6 fusion.53
  232.2 1.6 fusion.53
  239.9 1.6 fusion.53
  243.8 1.6 fusion.53
  247.7 1.6 fusion.53
  251.6 1.6 fusion.53
  255.5 1.6 fusion.53
  259.4 1.6 fusion.53
  263.3 1.6 fusion.53
  267.2 1.6 fusion.53
  271.1 1.6 fusion.53
  275.0 1.6 fusion.53
  278.9 1.6 fusion.53
  282.8 1.6 fusion.53
  286.7 1.6 fusion.53
  290.6 1.6 fusion.53
  294.5 1.6 fusion.53
  298.4 1.6 fusion.53
  641.6 5.9 fusion.22
  647.5 217.1 %while.31 = (s32[]{:T(128)}, f32[128,128]{1,0:T(8,128)S(1)}, f32[128,128]{1,0:T(8,128)S(1)}, s32[]{:T(128)}, s32[]{:T(128)}, /*index=5*/s32[]{:T(128)}) while((s32[]{:T(128)}, f32[128,128]{1,0:T(8,128)S(1)}, f32[128,128]{1,0:T(8,128)S(1)}, s32[]{:T(128)}, s32[]{:T(128)}, /*index=5*/s32[]{:T(128)}) %tuple.89), condition=%wide.region_6.0_spmd.clone, body=%wide.region_4.0_spmd.clone.sunk | while | flops 460035 | bytes 265336 | solution.py:43
  865.3 2.1 broadcast_multiply_fusion
  867.7 6.8 bitcast_subtract_fusion
  874.5 5.3 copy.7
  (1000 shorter events, 560.0 us)
Async XLA Ops:
  8.0 134.5 %all-reduce.3.cloned.1.call-start = ((), (), s32[]{:S(2)}) async-start(), calls=%async_computation | async-start | bytes 131072 | tf_op jit(solution)/shard_map/psum | solution.py:52
  10.3 631.3 %all-gather.2.cloned.1.call-start = ((), (), s32[]{:S(2)}) async-start(), calls=%async_computation.1 | async-start | bytes 1310720 | tf_op jit(solution)/shard_map/all_gather | solution.py:49
  10.9 854.4 %all-reduce.5.cloned.1.call-start = ((), (), s32[]{:S(2)}) async-start(), calls=%async_computation.2 | async-start | bytes 524288 | tf_op jit(solution)/shard_map/psum | solution.py:50
  641.6 226.1 %copy-start = (f32[2048,128]{1,0:T(8,128)S(1)}, f32[2048,128]{1,0:T(8,128)}, u32[]{:S(2)}) copy-start(f32[2048,128]{1,0:T(8,128)} %all-gather.2.cloned.1.call-done) | copy-start | bytes 3145732
Sparse Core Ops, SparseCore 0:
  15.0 127.4 all-reduce.2
Sparse Core Ops, SparseCore 1:
  12.4 19.0 all-gather.1
  647.6 68.7 all-reduce.4
where the time goes:
time: 902 us; the launch traced here: 887 us
  matrix products  425 us (47%)
  other arithmetic  215 us (24%)
  waiting for transfers between devices  127 us (14%)
  loops' own time  94.2 us (10%)
  between operations  15.5 us (2%)
  local copies, waits for them, and re-layouts  10.8 us (1%)
    dot_general x128, matrix products, column_step(): column = jnp.dot(remaining, picker, precision=lax.Precision.HIGHEST)  209 us
    add x128, other arithmetic, column_step(): lower = lower + column[:, None] * picker[None, :]  199 us
    psum x1, waiting for transfers between devices, body(): gram = lax.psum(local_gram, ('row', 'col'))  126 us
    dot_general x128, matrix products, row_step(): jnp.dot(factor_row, inverse, precision=lax.Precision.HIGHEST)  102 us
    dot_general x128, matrix products, row_step(): factor_row = jnp.dot(picker, factor, precision=lax.Precision.HIGHEST)  96.5 us
    another operation x1, loops' own time, upper_factor(): remaining, lower = lax.fori_loop(0, width, column_step, start)  89.8 us
  transfers between devices with their start and end apart: 3, of which 1 were waited for; matrix products, arithmetic and copies ran while one was open for 71% of the time, Pallas kernels for 0%

commit v1 on v0

--- a/solution.py
+++ b/solution.py
@@ -49,7 +49,7 @@
     gathered = lax.all_gather(panel_block, "col", axis=0, tiled=True)
     cross = lax.psum(inner_rows(gathered, trailing), "row")
     local_gram = inner_rows(panel_block, panel_block)
-    gram = lax.psum(local_gram, ("row", "col"))
+    gram = jnp.sum(lax.all_gather(local_gram, ("row", "col")), axis=0)
     factor = upper_factor(gram)
     inverse = upper_inverse(factor)
     weights = jnp.dot(inverse.T, cross, precision=lax.Precision.HIGHEST)

time: 902 us -> 539 us (0.60); the launches traced: 887 us -> 537 us
  other arithmetic: 215 us -> 29.2 us
  matrix products: 425 us -> 317 us
  waiting for transfers between devices: 127 us -> 67.6 us
    add x128, other arithmetic: 199 us -> 11.7 us  [column_step(): lower = lower + column[:, None] * picker[None, :]]
    psum x1 -> x0, waiting for transfers between devices: 126 us -> none  [body(): gram = lax.psum(local_gram, ('row', 'col'))]
    dot_general x128, matrix products: 209 us -> 101 us  [column_step(): column = jnp.dot(remaining, picker, precision=lax.Precision.HIGHEST)]
    all_gather x0 -> x1, waiting for transfers between devices: none -> 53.8 us  [body(): gram = jnp.sum(lax.all_gather(local_gram, ('row', 'col')), axis=0)]
    all_gather x1, waiting for transfers between devices: 0.03 us -> 13.1 us  [body(): gathered = lax.all_gather(panel_block, 'col', axis=0, tiled=True)]
  transfers between devices with their start and end apart: 3 -> 3, of which waited for: 1 -> 2; matrix products, arithmetic and copies ran while one was open for 71% -> 64% of each run, Pallas kernels for 0% -> 0%
where the time goes in v1:
time: 539 us; the launch traced here: 537 us
  matrix products  317 us (59%)
  loops' own time  98.3 us (18%)
  waiting for transfers between devices  67.6 us (13%)
  other arithmetic  29.2 us (5%)
  between operations  13.8 us (3%)
  local copies, waits for them, and re-layouts  10.8 us (2%)
    dot_general x128, matrix products, row_step(): jnp.dot(factor_row, inverse, precision=lax.Precision.HIGHEST)  102 us
    dot_general x128, matrix products, column_step(): column = jnp.dot(remaining, picker, precision=lax.Precision.HIGHEST)  101 us
    dot_general x128, matrix products, row_step(): factor_row = jnp.dot(picker, factor, precision=lax.Precision.HIGHEST)  96.5 us
    another operation x1, loops' own time, upper_factor(): remaining, lower = lax.fori_loop(0, width, column_step, start)  93.8 us
    all_gather x1, waiting for transfers between devices, body(): gram = jnp.sum(lax.all_gather(local_gram, ('row', 'col')), axis=0)  53.8 us
    add x128, other arithmetic, row_step(): return inverse + picker[:, None] * new_row[None, :]  13.4 us
    all_gather x1, waiting for transfers between devices, body(): gathered = lax.all_gather(panel_block, 'col', axis=0, tiled=True)  13.1 us
    add x128, other arithmetic, column_step(): lower = lower + column[:, None] * picker[None, :]  11.7 us
  transfers between devices with their start and end apart: 3, of which 2 were waited for; matrix products, arithmetic and copies ran while one was open for 64% of the time, Pallas kernels for 0%

profile of v1, /device:TPU:1, one launch (start us, length us, event | category | flops | bytes accessed | tf_op | source)
XLA Modules:
  0.0 536.6 jit_solution(18069868754984066594)
XLA Ops:
  7.9 2.3 fusion.21
  10.3 5.3 copy.6
  15.6 13.1 %all-gather.4.cloned.1.call-done = f32[2048,128]{1,0:T(8,128)} async-done(((f32[512,128]{1,0:T(8,128)}), f32[2048,128]{1,0:T(8,128)}) %all-gather.4.cloned.1.call-update) | async-done | bytes 1048592 | tf_op jit(solution)/shard_map/all_gather | solution.py:49
  28.7 5.8 %fusion.22 = f32[128,512]{1,0:T(8,128)} fusion(f32[2048,128]{1,0:T(8,128)} %all-gather.4.cloned.1.call-done, f32[2048,512]{1,0:T(8,128)} %param.7), kind=kOutput, calls=%fused_computation.32 | convolution fusion | flops 1610612736 | bytes 5505024 | tf_op jit(solution)/shard_map/rk,rc->kc/dot_general | solution.py:9
  34.6 53.8 %all-gather.6.cloned.1.call-done = f32[4096,128]{1,0:T(8,128)} async-done(((f32[128,128]{1,0:T(8,128)}), f32[4096,128]{1,0:T(8,128)}) %all-gather.6.cloned.1.call-update) | async-done | bytes 2097168 | tf_op jit(solution)/shard_map/all_gather | solution.py:52
  88.4 1.7 reduce_sum.35
  90.1 207.6 %while.32 = (s32[]{:T(128)}, f32[128,128]{1,0:T(8,128)S(1)}, f32[128,128]{1,0:T(8,128)S(1)}, s32[]{:T(128)}, s32[]{:T(128)}) while((s32[]{:T(128)}, f32[128,128]{1,0:T(8,128)S(1)}, f32[128,128]{1,0:T(8,128)S(1)}, s32[]{:T(128)}, s32[]{:T(128)}) %tuple.77), condition=%wide.region_3.4_spmd.clone.clone, body=%wide.region_1.3_spmd.clone.clone.sunk | while | flops 279682 | bytes 330859 | solution.py:27
  297.8 217.1 %while.31 = (s32[]{:T(128)}, f32[128,128]{1,0:T(8,128)S(1)}, f32[128,128]{1,0:T(8,128)S(1)}, s32[]{:T(128)}, s32[]{:T(128)}, /*index=5*/s32[]{:T(128)}) while((s32[]{:T(128)}, f32[128,128]{1,0:T(8,128)S(1)}, f32[128,128]{1,0:T(8,128)S(1)}, s32[]{:T(128)}, s32[]{:T(128)}, /*index=5*/s32[]{:T(128)}) %tuple.89), condition=%wide.region_6.0_spmd.clone, body=%wide.region_4.0_spmd.clone.sunk | while | flops 460035 | bytes 265336 | solution.py:43
  298.5 0.8 fusion.49
  310.4 0.8 fusion.49
  313.8 0.8 fusion.49
  317.2 0.8 fusion.49
  320.6 0.8 fusion.49
  324.0 0.8 fusion.49
  327.4 0.8 fusion.49
  330.8 0.8 fusion.49
  342.6 0.8 fusion.49
  346.0 0.8 fusion.49
  349.4 0.8 fusion.49
  352.8 0.8 fusion.49
  356.2 0.8 fusion.49
  359.6 0.8 fusion.49
  363.0 0.8 fusion.49
  374.8 0.8 fusion.49
  378.2 0.8 fusion.49
  381.6 0.8 fusion.49
  385.0 0.8 fusion.49
  388.4 0.8 fusion.49
  391.8 0.8 fusion.49
  395.2 0.8 fusion.49
  407.1 0.8 fusion.49
  410.5 0.8 fusion.49
  413.8 0.8 fusion.49
  417.2 0.8 fusion.49
  420.6 0.8 fusion.49
  424.0 0.8 fusion.49
  427.4 0.8 fusion.49
  439.3 0.8 fusion.49
  442.7 0.8 fusion.49
  446.1 0.8 fusion.49
  449.5 0.8 fusion.49
  452.8 0.8 fusion.49
  456.2 0.8 fusion.49
  459.6 0.8 fusion.49
  471.5 0.8 fusion.49
  515.5 2.1 broadcast_multiply_fusion
  517.9 6.8 %bitcast_subtract_fusion = f32[2048,512]{0,1:T(8,128)} fusion(f32[2048,512]{0,1:T(8,128)} %copy.6, f32[128,512]{1,0:T(8,128)S(1)} %fusion.23, f32[2048,128]{1,0:T(8,128)S(1)} %copy-done), kind=kOutput, calls=%fused_computation.28 | convolution fusion | flops 1611661312 | bytes 9699328 | tf_op jit(solution)/shard_map/dot_general | solution.py:57
  524.7 5.3 copy.7
  (1001 shorter events, 298.7 us)
Async XLA Ops:
  7.2 21.6 %all-gather.4.cloned.1.call-start = ((), (), s32[]{:S(2)}) async-start(), calls=%async_computation | async-start | bytes 1310720 | tf_op jit(solution)/shard_map/all_gather | solution.py:49
  7.9 80.5 %all-gather.6.cloned.1.call-start = ((), (), s32[]{:S(2)}) async-start(), calls=%async_computation.2 | async-start | bytes 2162688 | tf_op jit(solution)/shard_map/all_gather | solution.py:52
  10.2 505.2 %all-reduce.2.cloned.1.call-start = ((), (), s32[]{:S(2)}) async-start(), calls=%async_computation.1 | async-start | bytes 524288 | tf_op jit(solution)/shard_map/psum | solution.py:50
  34.5 483.4 %copy-start = (f32[2048,128]{1,0:T(8,128)S(1)}, f32[2048,128]{1,0:T(8,128)}, u32[]{:S(2)}) copy-start(f32[2048,128]{1,0:T(8,128)} %all-gather.4.cloned.1.call-done) | copy-start | bytes 3145732
Sparse Core Ops, SparseCore 0:
  9.5 19.1 all-gather.3
  32.1 56.1 all-gather.5
  92.3 67.8 all-reduce.1
